TPU v7x, 128 devices: a whole 4x4x4 slice. The times are simulated.
128 devices in a mesh: rows: 8 (over z, core), cols: 16 (over x, y).
Axes of the slice: x: 4, y: 4, z: 4, core: 2. Of those that a mesh axis runs over, the one named last changes fastest.
Arguments:
- pixels: bfloat16 [3, 1024, 4096], P(None, 'rows', 'cols'), may hold values from -6 to 6
- patch_weight: bfloat16 [48, 256], replicated, may hold values from -0.875 to 0.875
- patch_bias: float32 [256], replicated, may hold values from -4 to 4
- conv_kernel: float32 [49, 256], replicated, may hold values from -0.875 to 0.875
- norm_gain: float32 [256], replicated, may hold values from 0.1 to 1.9
- kv_weight: bfloat16 [256, 2048], replicated, may hold values from -0.375 to 0.375
- latents: bfloat16 [256, 1024], replicated, may hold values from -80 to 80, as said below
- d_attended: bfloat16 [256, 1024], replicated, may hold values from -6 to 6
Outputs:
- attended: float32 [256, 1024], replicated
- grad_latents: float32 [256, 1024], replicated
- grad_kv_weight: float32 [256, 2048], replicated
- grad_norm_gain: float32 [256], replicated
- grad_conv_kernel: float32 [49, 256], replicated
- grad_patch_weight: float32 [48, 256], replicated
- grad_patch_bias: float32 [256], replicated
Inputs may be any that keep to these rules, and one draw needn't show every extreme that they name: `latents`: each latent row has its own scale.
All inputs are finite; a program needn't handle non-finite values.
Results may differ from a plain program's by a relative error of at most 0.035.
The roundings to bfloat16 on the way count: a program that leaves them out, or rounds other values in their place, can miss the bound.
Values may be sent and summed in bfloat16 or wider, within the bound.
No kernel may reach another device: no remote copies, remote signals or barrier semaphores. Data moves between devices by JAX's collectives and lax.ppermute only.
A program may use at most 576 MiB of HBM per device.

v0:
```python
import jax
import jax.numpy as jnp
from jax import lax
from jax.sharding import PartitionSpec as P

PATCH = 4
KSIZE = 7
HEADS = 8
norm_eps = 1e-05


def padded_2(x, sides, width):
    for axis, dim in sides:
        devices, length = (lax.axis_size(axis), x.shape[dim])
        up = [(i, (i + 1) % devices) for i in range(devices - 1)]
        down = [(j, i) for i, j in up]
        last = lax.slice_in_dim(x, length - width, length, axis=dim)
        leading = lax.slice_in_dim(x, 0, width, axis=dim)
        before = lax.ppermute(last, axis, up)
        after = lax.ppermute(leading, axis, down)
        x = jnp.concatenate([before, x, after], axis=dim)
    return x


def patch_rows(pixels):
    in_channels, height, image_width = pixels.shape
    blocks = pixels.reshape(in_channels, height // PATCH, PATCH, image_width // PATCH, PATCH)
    blocks = blocks.transpose(1, 3, 0, 2, 4)
    return blocks.reshape(height // PATCH * (image_width // PATCH), in_channels * PATCH * PATCH)


def depthwise(padded, kernel, tile_rows, tile_cols):
    result = jnp.zeros((tile_rows, tile_cols, kernel.shape[1]), jnp.float32)
    for offset_row in range(KSIZE):
        for offset_col in range(KSIZE):
            window = padded[
                offset_row : offset_row + tile_rows, offset_col : offset_col + tile_cols
            ].astype(jnp.float32)
            result = result + window * kernel[offset_row * KSIZE + offset_col]
    return result


def transposed(padded, kernel, tile_rows, tile_cols):
    result = jnp.zeros((tile_rows, tile_cols, kernel.shape[1]), jnp.float32)
    last = KSIZE - 1
    for offset_row in range(KSIZE):
        for offset_col in range(KSIZE):
            start_row = last - offset_row
            start_col = last - offset_col
            window = padded[
                start_row : start_row + tile_rows, start_col : start_col + tile_cols
            ].astype(jnp.float32)
            result = result + window * kernel[offset_row * KSIZE + offset_col]
    return result


def kernel_grad(padded, upstream, tile_rows, tile_cols):
    upstream_f = upstream.astype(jnp.float32)
    kernel_terms = []
    for offset_row in range(KSIZE):
        for offset_col in range(KSIZE):
            window = padded[
                offset_row : offset_row + tile_rows, offset_col : offset_col + tile_cols
            ].astype(jnp.float32)
            kernel_terms.append(jnp.sum(window * upstream_f, axis=(0, 1)))
    return jnp.stack(kernel_terms)


def normalize(mixed):
    centre = mixed - jnp.mean(mixed, axis=-1, keepdims=True)
    variance = jnp.mean(centre * centre, axis=-1, keepdims=True)
    inverse = lax.rsqrt(variance + norm_eps)
    return (centre * inverse, inverse)


def split_heads(matrix, head_count):
    return matrix.reshape(matrix.shape[0], head_count, -1).transpose(1, 0, 2)


def merge_heads(stacked):
    return stacked.transpose(1, 0, 2).reshape(stacked.shape[1], -1)


def head_state(pieces):
    queries, key_rows, values = pieces
    score_scale = queries.shape[-1] ** (-0.5)
    scores = (
        jnp.einsum("le,te->lt", queries, key_rows, preferred_element_type=jnp.float32) * score_scale
    )
    top_score = jnp.max(scores, axis=1)
    raised = jnp.exp(scores - top_score[:, None])
    weighted = jnp.dot(raised.astype(jnp.bfloat16), values, preferred_element_type=jnp.float32)
    return (top_score, jnp.sum(raised, axis=1), weighted)


def head_grads(pieces):
    queries, key_rows, values, top_score, sum_exp, row_dots, upstream = pieces
    score_scale = queries.shape[-1] ** (-0.5)
    scores = (
        jnp.einsum("le,te->lt", queries, key_rows, preferred_element_type=jnp.float32) * score_scale
    )
    probs = jnp.exp(scores - top_score[:, None]) / sum_exp[:, None]
    d_probs = jnp.einsum("le,te->lt", upstream, values, preferred_element_type=jnp.float32)
    d_scores = (probs * (d_probs - row_dots[:, None]) * score_scale).astype(jnp.bfloat16)
    q_grad = jnp.einsum("lt,te->le", d_scores, key_rows, preferred_element_type=jnp.float32)
    k_grad = jnp.einsum("lt,le->te", d_scores, queries, preferred_element_type=jnp.float32).astype(
        jnp.bfloat16
    )
    v_grad = jnp.einsum(
        "lt,le->te", probs.astype(jnp.bfloat16), upstream, preferred_element_type=jnp.float32
    )
    return (q_grad, k_grad, v_grad.astype(jnp.bfloat16))


def rescaled(local_top, local_sum, local_weighted, top_score):
    factor = jnp.exp(local_top - top_score)
    latent_count, head_count = factor.shape
    weighted = local_weighted.reshape(latent_count, head_count, -1) * factor[:, :, None]
    return (local_sum * factor, weighted.reshape(latent_count, -1))


def normalized(weighted, sum_exp):
    latent_count, head_count = sum_exp.shape
    return (weighted.reshape(latent_count, head_count, -1) / sum_exp[:, :, None]).reshape(
        latent_count, -1
    )


def per_device(
    pixels, patch_weight, patch_bias, conv_kernel, norm_gain, kv_weight, latents, d_attended
):
    tile_rows = pixels.shape[1] // PATCH
    tile_cols = pixels.shape[2] // PATCH
    channels = patch_weight.shape[1]
    model_dim = latents.shape[1]
    latent_count = latents.shape[0]
    patches = patch_rows(pixels)
    embedded = (
        jnp.dot(patches, patch_weight, preferred_element_type=jnp.float32) + patch_bias
    ).astype(jnp.bfloat16)
    embedded = embedded.reshape(tile_rows, tile_cols, channels)
    padded = padded_2(embedded, (("rows", 0), ("cols", 1)), KSIZE // 2)
    mixed = embedded.astype(jnp.float32) + depthwise(padded, conv_kernel, tile_rows, tile_cols)
    centred, inverse = normalize(mixed)
    normed = (centred * norm_gain).astype(jnp.bfloat16).reshape(tile_rows * tile_cols, channels)
    projected = jnp.dot(normed, kv_weight, preferred_element_type=jnp.float32).astype(jnp.bfloat16)
    query_heads = split_heads(latents, HEADS)
    key_heads = split_heads(projected[:, :model_dim], HEADS)
    value_heads = split_heads(projected[:, model_dim:], HEADS)
    tops, sums, weighteds = lax.map(head_state, (query_heads, key_heads, value_heads))
    local_top = tops.T
    local_sum = sums.T
    local_weighted = merge_heads(weighteds)
    top_score = lax.pmax(local_top, ("rows", "cols"))
    part_sum, part_weighted = rescaled(local_top, local_sum, local_weighted, top_score)
    sum_exp, weighted = lax.psum((part_sum, part_weighted), ("rows", "cols"))
    attended = normalized(weighted, sum_exp)
    row_dots = jnp.sum(
        d_attended.astype(jnp.float32).reshape(latent_count, HEADS, -1)
        * attended.reshape(latent_count, HEADS, -1),
        axis=2,
    )
    q_grads, k_grads, v_grads = lax.map(
        head_grads,
        (
            query_heads,
            key_heads,
            value_heads,
            top_score.T,
            sum_exp.T,
            row_dots.T,
            split_heads(d_attended, HEADS),
        ),
    )
    local_latents = merge_heads(q_grads)
    d_projected = jnp.concatenate([merge_heads(k_grads), merge_heads(v_grads)], axis=1)
    local_kv = jnp.einsum("tc,tk->ck", normed, d_projected, preferred_element_type=jnp.float32)
    d_normed = jnp.einsum("tk,ck->tc", d_projected, kv_weight, preferred_element_type=jnp.float32)
    d_normed = d_normed.reshape(tile_rows, tile_cols, channels)
    local_gain = jnp.sum(d_normed * centred, axis=(0, 1))
    scaled = d_normed * norm_gain
    d_mixed = inverse * (
        scaled
        - jnp.mean(scaled, axis=-1, keepdims=True)
        - centred * jnp.mean(scaled * centred, axis=-1, keepdims=True)
    )
    d_mixed = d_mixed.astype(jnp.bfloat16)
    local_kernel = kernel_grad(padded, d_mixed, tile_rows, tile_cols)
    d_padded = padded_2(d_mixed, (("rows", 0), ("cols", 1)), KSIZE // 2)
    d_embedded = (
        d_mixed.astype(jnp.float32) + transposed(d_padded, conv_kernel, tile_rows, tile_cols)
    ).astype(jnp.bfloat16)
    d_embedded = d_embedded.reshape(tile_rows * tile_cols, channels)
    local_patch = jnp.einsum("tp,tc->pc", patches, d_embedded, preferred_element_type=jnp.float32)
    local_bias = jnp.sum(d_embedded.astype(jnp.float32), axis=0)
    grad_latents, grad_kv, grad_gain, grad_kernel, grad_patch, grad_bias = lax.psum(
        (local_latents, local_kv, local_gain, local_kernel, local_patch, local_bias),
        ("rows", "cols"),
    )
    return (attended, grad_latents, grad_kv, grad_gain, grad_kernel, grad_patch, grad_bias)


def solution(mesh):
    return jax.shard_map(
        per_device,
        mesh=mesh,
        in_specs=(P(None, "rows", "cols"), P(), P(), P(), P(), P(), P(), P()),
        out_specs=(P(), P(), P(), P(), P(), P(), P()),
        check_vma=False,
    )
```

profile of v0, /device:TPU:1, one launch (start us, length us, event | category | flops | bytes accessed | tf_op | source)
XLA Modules:
  0.0 872.1 jit_solution(149863310632694244)
XLA Ops:
  7.2 15.3 %reshape.154 = bf16[3,32,4,64,4]{4,3,2,1,0:T(8,128)(2,1)} reshape(bf16[3,128,256]{2,1,0:T(8,128)(2,1)} %param.12) | data formatting | bytes 393216 | tf_op jit(solution)/shard_map/reshape | solution.py:27
  22.6 6.0 copy.22
  29.5 3.3 collective-permute-start.1
  32.8 3.5 collective-permute-start
  38.1 3.2 collective-permute-start.2
  48.9 19.2 %fusion.180 = (f32[32,64]{1,0:T(8,128)S(1)}, f32[32,64,256]{2,1,0:T(8,128)S(1)}) fusion(f32[256]{0:T(256)} %bitcast.382, bf16[38,67,256]{2,1,0:T(8,128)(2,1)S(1)} %get-tuple-element.249, f32[256]{0:T(256)} %bitcast.384, f32[256]{0:T(256)S(1)} %bitcast.290, f32[256]{0:T(256)S(1)} %bitcast.292, bf16[3,64,256]{2,1,0:T(8,128)(2,1)S(1)} %copy-done.16, ...), kind=kLoop, calls=%fused_computation.344 | loop fusion | flops 80738304 | bytes 47440896 | tf_op jit(solution)/shard_map/reduce_sum | solution.py:70
  69.6 2.4 convolution_convert_fusion.2
  72.0 3.6 fusion.182
  75.6 6.4 copy.24
  82.0 6.4 copy.23
  88.6 39.8 %while.28 = (s32[]{:T(128)}, f32[8,256]{1,0:T(8,128)S(1)}, f32[8,256]{1,0:T(8,128)}, f32[8,256,128]{2,1,0:T(8,128)S(1)}, bf16[8,256,128]{2,1,0:T(8,128)(2,1)}, /...) while((s32[]{:T(128)}, f32[8,256]{1,0:T(8,128)S(1)}, ...), condition=%wide.region_5.6_spmd, body=%wide.region_2.5_spmd.sunk | while | flops 271580672 | bytes 7546989 | solution.py:150
  128.9 69.0 %pmax.7 = f32[256,8]{0,1:T(8,128)S(1)} all-reduce(f32[256,8]{0,1:T(8,128)} %bitcast.284), channel_id=1, replica_groups=mesh['rows'=8,'cols'=16] {'rows','cols'}, use_global_device_ids=true, to_apply=%region_6.7 | all-reduce | flops 2048 | bytes 16384 | tf_op jit(solution)/shard_map/pmax | solution.py:154
  202.7 64.4 %psum.57 = f32[256,8]{0,1:T(8,128)S(1)} all-reduce(f32[256,8]{0,1:T(8,128)S(1)} %copy-done.32), channel_id=1, replica_groups=mesh['rows'=8,'cols'=16] {'rows','cols'}, use_global_device_ids=true, to_apply=%region_8.9 | all-reduce | flops 2048 | bytes 16384 | tf_op jit(solution)/shard_map/psum | solution.py:156
  267.1 78.4 %all-reduce.6.cloned.1.call-done = f32[256,1024]{1,0:T(8,128)} async-done(((f32[256,1024]{1,0:T(8,128)}), f32[256,1024]{1,0:T(8,128)}) %all-reduce.6.cloned.1.call-update) | async-done | bytes 1048592 | tf_op jit(solution)/shard_map/psum | solution.py:156
  350.0 126.1 %while.29 = (s32[]{:T(128)}, f32[8,256,128]{2,1,0:T(8,128)}, bf16[8,2048,128]{1,2,0:T(8,128)(2,1)}, bf16[8,2048,128]{1,2,0:T(8,128)(2,1)}, bf16[8,256,128]{2,1,0...) while((s32[]{:T(128)}, f32[8,256,128]{2,1,0:T(8,128)}, ...), condition=%wide.region_11.12_spmd, body=%wide.region_10.11_spmd.sunk | while | flops 675807232 | bytes 16658581 | solution.py:163
  352.3 2.1 fusion.238
  356.1 2.1 copy.46
  358.1 2.1 fusion.239
  360.3 2.1 fusion.237
  363.6 2.1 constant_dynamic-update-slice_fusion.3
  368.1 2.1 fusion.238
  371.9 2.1 copy.46
  373.9 2.1 fusion.239
  376.1 2.1 fusion.237
  379.4 2.2 constant_dynamic-update-slice_fusion.3
  384.0 2.1 fusion.238
  387.7 2.1 copy.46
  389.7 2.1 fusion.239
  391.9 2.1 fusion.237
  395.3 2.1 constant_dynamic-update-slice_fusion.3
  399.7 2.1 fusion.238
  405.5 2.1 fusion.239
  407.6 2.1 fusion.237
  411.0 2.1 constant_dynamic-update-slice_fusion.3
  415.4 2.1 fusion.238
  421.2 2.1 fusion.239
  423.4 2.1 fusion.237
  426.7 2.1 constant_dynamic-update-slice_fusion.3
  431.2 2.1 fusion.238
  437.0 2.1 fusion.239
  439.1 2.1 fusion.237
  442.5 2.1 constant_dynamic-update-slice_fusion.3
  447.0 2.1 fusion.238
  452.8 2.1 fusion.239
  454.9 2.1 fusion.237
  458.3 2.1 constant_dynamic-update-slice_fusion.3
  462.7 2.1 fusion.238
  468.5 2.1 fusion.239
  470.6 2.1 fusion.237
  474.0 2.1 constant_dynamic-update-slice_fusion.3
  476.1 7.3 multiply_reduce_fusion.1
  484.1 4.5 multiply_reduce_fusion
  488.6 6.6 fusion.137
  495.3 6.5 fusion.141
  501.7 2.9 collective-permute-start.4
  504.7 2.4 collective-permute-start.5
  507.1 5.6 fusion.140
  512.8 8.2 fusion.43
  523.1 4.6 collective-permute-start.7
  529.4 9.1 %stack.199 = f32[49,256]{1,0:T(8,128)} concatenate(f32[1,256]{1,0:T(1,128)} %bitcast.434, f32[1,256]{1,0:T(1,128)} %bitcast.433, f32[1,256]{1,0:T(1,128)} %bitcast.432, f32[1,256]{1,0:T(1,128)} %bitcast.428, f32[1,256]{1,0:T(1,128)} %bitcast.424, f32[1,256]{1,0:T(1,128)} %bitcast.423, f32[1,256]{1,0:T(1,128)} %bitcast.405, f32[1,256]{1,0:T(1,128)S(1)} %bitcast.387, ...), dimensions={0} | concatenate | bytes 100352 | tf_op jit(solution)/shard_map/stack | solution.py:66
  541.0 21.4 %convert_reduce_fusion = (f32[256]{0:T(256)}, bf16[32,64,256]{2,1,0:T(8,128)(2,1)S(1)}) fusion(f32[256]{0:T(256)} %bitcast.383, bf16[38,67,256]{2,1,0:T(8,128)(2,1)S(1)} %get-tuple-element.245, f32[256]{0:T(256)} %bitcast.385, f32[256]{0:T(256)S(1)} %bitcast.291, f32[256]{0:T(256)S(1)} %bitcast.293, bf16[32,64,256]{2,1,0:T(8,128)(2,1)S(1)} %get-tuple-element.233, ...), kind=kLoop, calls=%fused_computation.283 | loop fusion | flops 81788672 | bytes 46385152 | tf_op jit(solution)/shard_map/reduce_sum | solution.py:195
  568.5 135.2 %all-reduce.8.cloned.1.call-done = (f32[256]{0:T(256)}, f32[49,256]{1,0:T(8,128)}, f32[48,256]{1,0:T(8,128)}, f32[256]{0:T(256)}) async-done(((f32[256]{0:T(256)}, f32[49,256]{1,0:T(8,128)}, f32[48,256]{1,0:T(8,128)}, f32[256]{0:T(256)}), (f32[256]{0:T(256)}, f32[49,256]{1,0:T(8,128)}, f32[48,256]{1,0:T(8,128)}, f32[256]{0:T(256)})) %all-reduce.8.cloned.1.call-update) | async-done | bytes 101392 | tf_op jit(solution)/shard_map/psum | solution.py:196
  703.7 155.7 %all-reduce.10.cloned.1.call-done = (f32[256,1024]{1,0:T(8,128)}, f32[256,2048]{1,0:T(8,128)}) async-done(((f32[256,1024]{1,0:T(8,128)}, f32[256,2048]{1,0:T(8,128)}), (f32[256,1024]{1,0:T(8,128)}, f32[256,2048]{1,0:T(8,128)})) %all-reduce.10.cloned.1.call-update) | async-done | bytes 3145744 | tf_op jit(solution)/shard_map/psum | solution.py:196
  859.4 2.5 copy.87
  (399 shorter events, 128.1 us)
Async XLA Ops:
  7.2 62.4 %copy-start = (bf16[256,2048]{1,0:T(8,128)(2,1)S(1)}, bf16[256,2048]{1,0:T(8,128)(2,1)}, u32[]{:S(2)}) copy-start(bf16[256,2048]{1,0:T(8,128)(2,1)} %param.17) | copy-start | bytes 3145732
  7.2 338.3 %all-reduce.6.cloned.1.call-start = ((), (), s32[]{:S(2)}) async-start(), calls=%async_computation | async-start | bytes 2097152 | tf_op jit(solution)/shard_map/psum | solution.py:156
  22.6 6.4 copy-start.33
  22.6 6.4 copy-start.121
  28.6 7.8 copy-start.30
  28.6 14.8 %copy-start.25 = (bf16[256,1024]{1,0:T(8,128)(2,1)S(1)}, bf16[256,1024]{1,0:T(8,128)(2,1)}, u32[]{:S(2)}) copy-start(bf16[256,1024]{1,0:T(8,128)(2,1)} %param.18) | copy-start | bytes 1572868
  29.0 14.4 %copy-start.13 = (bf16[2048,48]{0,1:T(8,128)(2,1)}, bf16[2048,48]{0,1:T(8,128)(2,1)S(1)}, u32[]{:S(2)}) copy-start(bf16[2048,48]{0,1:T(8,128)(2,1)S(1)} %reshape.155) | copy-start | bytes 589828
  29.5 19.1 %copy-start.5 = (bf16[2048,256]{1,0:T(8,128)(2,1)}, bf16[2048,256]{1,0:T(8,128)(2,1)S(1)}, u32[]{:S(2)}) copy-start(bf16[2048,256]{1,0:T(8,128)(2,1)S(1)} %fusion.44) | copy-start | bytes 3145732
  29.5 8.2 collective-permute-start.1
  32.8 5.2 collective-permute-start
  37.7 5.7 copy-start.15
  38.0 5.4 copy-start.18
  38.1 6.9 collective-permute-start.2
  41.3 5.6 collective-permute-start.3
  44.7 3.9 copy-start.37
  44.7 3.9 copy-start.39
  44.7 3.9 copy-start.41
  44.7 3.9 copy-start.43
  44.7 3.9 copy-start.45
  44.7 3.9 copy-start.47
  44.7 3.9 copy-start.49
  44.7 3.9 copy-start.51
  44.7 3.9 copy-start.53
  44.7 3.9 copy-start.55
  44.8 3.9 copy-start.57
  44.8 3.9 copy-start.59
  44.8 3.9 copy-start.61
  44.8 3.9 copy-start.63
  44.8 3.9 copy-start.65
  44.8 3.9 copy-start.67
  44.8 3.9 copy-start.69
  44.8 3.9 copy-start.71
  44.8 3.9 copy-start.73
  44.8 3.9 copy-start.75
  48.5 19.6 %copy-start.1 = (bf16[38,67,256]{2,1,0:T(8,128)(2,1)}, bf16[38,67,256]{2,1,0:T(8,128)(2,1)S(1)}, u32[]{:S(2)}) copy-start(bf16[38,67,256]{2,1,0:T(8,128)(2,1)S(1)} %get-tuple-element.249) | copy-start | bytes 3910660
  200.6 503.2 %all-reduce.8.cloned.1.call-start = ((), (), s32[]{:S(2)}) async-start(), calls=%async_computation.1 | async-start | bytes 217088 | tf_op jit(solution)/shard_map/psum | solution.py:196
  476.1 8.0 copy-start.109
  484.1 4.5 copy-start.4
  484.1 4.5 copy-start.7
  484.1 4.5 copy-start.27
  488.6 6.6 copy-start.2
  495.2 11.9 %copy-start.6 = (bf16[2048,256]{1,0:T(8,128)(2,1)S(1)}, bf16[2048,256]{1,0:T(8,128)(2,1)}, u32[]{:S(2)}) copy-start(bf16[2048,256]{1,0:T(8,128)(2,1)} %copy-done.5) | copy-start | bytes 3145732
  495.2 11.9 %copy-start.17 = (bf16[3,64,256]{2,1,0:T(8,128)(2,1)S(1)}, bf16[3,64,256]{2,1,0:T(8,128)(2,1)}, u32[]{:S(2)}) copy-start(bf16[3,64,256]{2,1,0:T(8,128)(2,1)} %copy-done.15) | copy-start | bytes 294916
  495.2 11.9 %copy-start.20 = (bf16[3,64,256]{2,1,0:T(8,128)(2,1)S(1)}, bf16[3,64,256]{2,1,0:T(8,128)(2,1)}, u32[]{:S(2)}) copy-start(bf16[3,64,256]{2,1,0:T(8,128)(2,1)} %copy-done.18) | copy-start | bytes 294916
  495.2 17.5 %copy-start.123 = (bf16[8,2048,128]{1,2,0:T(8,128)(2,1)S(1)}, bf16[8,2048,128]{1,2,0:T(8,128)(2,1)}, u32[]{:S(2)}) copy-start(bf16[8,2048,128]{1,2,0:T(8,128)(2,1)} %get-tuple-element.109) | copy-start | bytes 12582916
  501.7 19.3 %collective-permute-start.4 = (bf16[3,64,256]{2,1,0:T(8,128)(2,1)S(1)}, bf16[3,64,256]{2,1,0:T(8,128)(2,1)S(1)}, u32[]{:S(2)}, u32[]{:S(2)}) collective-permute-start(bf16[3,64,256]{2,1,0:T(8,128)(2,1)S(1)} %get-tuple-element.252), channel_id=1, source_target_pairs={{0,16},{16,32},{32,48},{48,64},{64,80},{80,96},{96,112},{1,17},{17... | collective-permute-start | bytes 294920 | tf_op jit(solution)/shard_map/ppermute | solution.py:19
  504.6 8.1 copy-start.9
  504.6 8.1 copy-start.122
  504.7 16.4 %collective-permute-start.5 = (bf16[3,64,256]{2,1,0:T(8,128)(2,1)S(1)}, bf16[3,64,256]{2,1,0:T(8,128)(2,1)S(1)}, u32[]{:S(2)}, u32[]{:S(2)}) collective-permute-start(bf16[3,64,256]{2,1,0:T(8,128)(2,1)S(1)} %get-tuple-element.253), channel_id=1, source_target_pairs={{16,0},{32,16},{48,32},{64,48},{80,64},{96,80},{112,96},{17,1},{33... | collective-permute-start | bytes 294920 | tf_op jit(solution)/shard_map/ppermute | solution.py:20
  521.0 8.3 copy-start.21
  521.0 8.3 copy-start.23
  521.8 17.1 %collective-permute-start.6 = (bf16[38,3,256]{2,1,0:T(4,128)(2,1)}, bf16[38,3,256]{2,1,0:T(4,128)(2,1)}, u32[]{:S(2)}, u32[]{:S(2)}) collective-permute-start(bf16[38,3,256]{2,1,0:T(4,128)(2,1)} %get-tuple-element.246), channel_id=1, source_target_pairs={{1,0},{2,1},{3,2},{4,3},{5,4},{6,5},{7,6},{8,7},{9,8},{10,9},{11,1... | collective-permute-start | bytes 175112 | tf_op jit(solution)/shard_map/ppermute | solution.py:20
  523.0 6.2 copy-start.110
  523.1 6.2 copy-start.111
  523.1 6.2 copy-start.112
  523.1 6.2 copy-start.113
  523.1 6.2 copy-start.114
  523.1 6.2 copy-start.115
  523.1 6.2 copy-start.116
  523.1 6.2 copy-start.117
  523.1 6.2 copy-start.118
  523.1 15.7 %collective-permute-start.7 = (bf16[38,3,256]{2,1,0:T(4,128)(2,1)}, bf16[38,3,256]{2,1,0:T(4,128)(2,1)}, u32[]{:S(2)}, u32[]{:S(2)}) collective-permute-start(bf16[38,3,256]{2,1,0:T(4,128)(2,1)} %get-tuple-element.247), channel_id=1, source_target_pairs={{0,1},{1,2},{2,3},{3,4},{4,5},{5,6},{6,7},{7,8},{8,9},{9,10},{10,1... | collective-permute-start | bytes 175112 | tf_op jit(solution)/shard_map/ppermute | solution.py:19
  541.0 21.4 %copy-start.14 = (bf16[2048,48]{0,1:T(8,128)(2,1)S(1)}, bf16[2048,48]{0,1:T(8,128)(2,1)}, u32[]{:S(2)}) copy-start(bf16[2048,48]{0,1:T(8,128)(2,1)} %copy-done.13) | copy-start | bytes 589828
  563.3 296.1 %all-reduce.10.cloned.1.call-start = ((), (), s32[]{:S(2)}) async-start(), calls=%async_computation.2 | async-start | bytes 6291456 | tf_op jit(solution)/shard_map/psum | solution.py:196
  (71 other events, 180.0 us)
Sparse Core Ops, SparseCore 0:
  200.7 144.7 all-reduce.5
  563.4 140.2 all-reduce.7
  709.1 150.2 all-reduce.9
where the time goes:
time: 877 us; the launch traced here: 872 us
  waiting for transfers between devices  371 us (42%)
  blocking collectives  133 us (15%)
  local copies, waits for them, and re-layouts  128 us (15%)
  matrix products  122 us (14%)
  other arithmetic  79.9 us (9%)
  starting transfers between devices  22.9 us (3%)
  between operations  15.6 us (2%)
    psum x2, waiting for transfers between devices, per_device(): lax.psum((local_latents, local_kv, local_gain, local_kernel, local_patch,...  291 us
    psum x1, waiting for transfers between devices, per_device(): sum_exp, weighted = lax.psum((part_sum, part_weighted), ('rows', 'cols'))  78.4 us
    pmax x1, blocking collectives, per_device(): top_score = lax.pmax(local_top, ('rows', 'cols'))  69 us
    psum x1, blocking collectives, per_device(): sum_exp, weighted = lax.psum((part_sum, part_weighted), ('rows', 'cols'))  64.4 us
    dynamic_update_slice x24, local copies, waits for them, and re-layouts, per_device(): lax.map(head_grads, (query_heads, key_heads, value_heads, top_score.T, su...  43.4 us
    reduce_sum x1, other arithmetic, per_device(): local_bias = jnp.sum(d_embedded.astype(jnp.float32), axis=0)  21.4 us
    reduce_sum x4, other arithmetic, kernel_grad(): kernel_terms.append(jnp.sum(window * upstream_f, axis=(0, 1)))  20.2 us
    reduce_sum x1, other arithmetic, normalize(): centre = mixed - jnp.mean(mixed, axis=-1, keepdims=True)  19.2 us
  transfers between devices with their start and end apart: 11, of which 5 were waited for; matrix products, arithmetic and copies ran while one was open for 4% of the time, Pallas kernels for 0%

commit v1 on v0

--- a/solution.py
+++ b/solution.py
@@ -2,6 +2,7 @@
 import jax.numpy as jnp
 from jax import lax
 from jax.sharding import PartitionSpec as P
+from jax.lax import psum
 
 PATCH = 4
 KSIZE = 7
@@ -193,9 +194,14 @@
     d_embedded = d_embedded.reshape(tile_rows * tile_cols, channels)
     local_patch = jnp.einsum("tp,tc->pc", patches, d_embedded, preferred_element_type=jnp.float32)
     local_bias = jnp.sum(d_embedded.astype(jnp.float32), axis=0)
-    grad_latents, grad_kv, grad_gain, grad_kernel, grad_patch, grad_bias = lax.psum(
-        (local_latents, local_kv, local_gain, local_kernel, local_patch, local_bias),
-        ("rows", "cols"),
+
+    def _solve_trails(original, axis_key, device_axis="rows"):
+        for at in (axis_key, device_axis):
+            original = psum(original, at)
+        return original
+
+    grad_latents, grad_kv, grad_gain, grad_kernel, grad_patch, grad_bias = _solve_trails(
+        (local_latents, local_kv, local_gain, local_kernel, local_patch, local_bias), "cols"
     )
     return (attended, grad_latents, grad_kv, grad_gain, grad_kernel, grad_patch, grad_bias)
 

time: 877 us -> 893 us (1.018)
  waiting for transfers between devices: 371 us -> 385 us
    psum x2 -> x4, waiting for transfers between devices: 291 us -> 305 us  [_solve_trails(): original = psum(original, at)]
  transfers between devices with their start and end apart: 11 -> 13, of which waited for: 5 -> 7; matrix products, arithmetic and copies ran while one was open for 4% -> 4% of each run, Pallas kernels for 0% -> 0%
where the time goes in v1:
time: 893 us; the launch traced here: 887 us
  waiting for transfers between devices  385 us (43%)
  blocking collectives  133 us (15%)
  local copies, waits for them, and re-layouts  128 us (14%)
  matrix products  122 us (14%)
  other arithmetic  79.9 us (9%)
  starting transfers between devices  23 us (3%)
  between operations  15.6 us (2%)
    psum x4, waiting for transfers between devices, _solve_trails(): original = psum(original, at)  305 us
    psum x1, waiting for transfers between devices, per_device(): sum_exp, weighted = lax.psum((part_sum, part_weighted), ('rows', 'cols'))  78.4 us
    pmax x1, blocking collectives, per_device(): top_score = lax.pmax(local_top, ('rows', 'cols'))  69 us
    psum x1, blocking collectives, per_device(): sum_exp, weighted = lax.psum((part_sum, part_weighted), ('rows', 'cols'))  64.4 us
    dynamic_update_slice x24, local copies, waits for them, and re-layouts, per_device(): lax.map(head_grads, (query_heads, key_heads, value_heads, top_score.T, su...  43.4 us
    reduce_sum x1, other arithmetic, per_device(): local_bias = jnp.sum(d_embedded.astype(jnp.float32), axis=0)  21.4 us
    reduce_sum x4, other arithmetic, kernel_grad(): kernel_terms.append(jnp.sum(window * upstream_f, axis=(0, 1)))  20.2 us
    reduce_sum x1, other arithmetic, normalize(): centre = mixed - jnp.mean(mixed, axis=-1, keepdims=True)  19.2 us
  transfers between devices with their start and end apart: 13, of which 7 were waited for; matrix products, arithmetic and copies ran while one was open for 4% of the time, Pallas kernels for 0%

profile of v1, /device:TPU:1, one launch (start us, length us, event | category | flops | bytes accessed | tf_op | source)
XLA Modules:
  0.0 886.7 jit_solution(7710292637918321966)
XLA Ops:
  7.2 15.3 %reshape.154 = bf16[3,32,4,64,4]{4,3,2,1,0:T(8,128)(2,1)} reshape(bf16[3,128,256]{2,1,0:T(8,128)(2,1)} %param.12) | data formatting | bytes 393216 | tf_op jit(solution)/shard_map/reshape | solution.py:28
  22.6 6.0 copy.22
  29.5 3.3 collective-permute-start.1
  32.8 3.5 collective-permute-start
  38.1 3.2 collective-permute-start.2
  48.9 19.2 %fusion.180 = (f32[32,64]{1,0:T(8,128)S(1)}, f32[32,64,256]{2,1,0:T(8,128)S(1)}) fusion(f32[256]{0:T(256)} %bitcast.382, bf16[38,67,256]{2,1,0:T(8,128)(2,1)S(1)} %get-tuple-element.255, f32[256]{0:T(256)} %bitcast.384, f32[256]{0:T(256)S(1)} %bitcast.290, f32[256]{0:T(256)S(1)} %bitcast.292, bf16[3,64,256]{2,1,0:T(8,128)(2,1)S(1)} %copy-done.16, ...), kind=kLoop, calls=%fused_computation.344 | loop fusion | flops 80738304 | bytes 47440896 | tf_op jit(solution)/shard_map/reduce_sum | solution.py:71
  69.6 2.4 convolution_convert_fusion.2
  72.0 3.6 fusion.182
  75.6 6.4 copy.24
  82.0 6.4 copy.23
  88.6 39.8 %while.28 = (s32[]{:T(128)}, f32[8,256]{1,0:T(8,128)S(1)}, f32[8,256]{1,0:T(8,128)}, f32[8,256,128]{2,1,0:T(8,128)S(1)}, bf16[8,256,128]{2,1,0:T(8,128)(2,1)}, /...) while((s32[]{:T(128)}, f32[8,256]{1,0:T(8,128)S(1)}, ...), condition=%wide.region_5.6_spmd, body=%wide.region_2.5_spmd.sunk | while | flops 271580672 | bytes 7546989 | solution.py:151
  128.9 69.0 %pmax.7 = f32[256,8]{0,1:T(8,128)S(1)} all-reduce(f32[256,8]{0,1:T(8,128)} %bitcast.284), channel_id=1, replica_groups=mesh['rows'=8,'cols'=16] {'rows','cols'}, use_global_device_ids=true, to_apply=%region_6.7 | all-reduce | flops 2048 | bytes 16384 | tf_op jit(solution)/shard_map/pmax | solution.py:155
  202.7 64.4 %psum.99 = f32[256,8]{0,1:T(8,128)S(1)} all-reduce(f32[256,8]{0,1:T(8,128)S(1)} %copy-done.32), channel_id=1, replica_groups=mesh['rows'=8,'cols'=16] {'rows','cols'}, use_global_device_ids=true, to_apply=%region_8.9 | all-reduce | flops 2048 | bytes 16384 | tf_op jit(solution)/shard_map/psum | solution.py:157
  267.1 78.4 %all-reduce.10.cloned.1.call-done = f32[256,1024]{1,0:T(8,128)} async-done(((f32[256,1024]{1,0:T(8,128)}), f32[256,1024]{1,0:T(8,128)}) %all-reduce.10.cloned.1.call-update) | async-done | bytes 1048592 | tf_op jit(solution)/shard_map/psum | solution.py:157
  350.0 126.1 %while.29 = (s32[]{:T(128)}, f32[8,256,128]{2,1,0:T(8,128)}, bf16[8,2048,128]{1,2,0:T(8,128)(2,1)}, bf16[8,2048,128]{1,2,0:T(8,128)(2,1)}, bf16[8,256,128]{2,1,0...) while((s32[]{:T(128)}, f32[8,256,128]{2,1,0:T(8,128)}, ...), condition=%wide.region_11.12_spmd, body=%wide.region_10.11_spmd.sunk | while | flops 675807232 | bytes 16658581 | solution.py:164
  352.3 2.1 fusion.238
  356.1 2.1 copy.46
  358.1 2.1 fusion.239
  360.3 2.1 fusion.237
  363.6 2.1 constant_dynamic-update-slice_fusion.3
  368.1 2.1 fusion.238
  373.9 2.1 fusion.239
  376.1 2.1 fusion.237
  379.4 2.2 constant_dynamic-update-slice_fusion.3
  384.0 2.1 fusion.238
  389.7 2.1 fusion.239
  391.9 2.1 fusion.237
  395.3 2.1 constant_dynamic-update-slice_fusion.3
  399.7 2.1 fusion.238
  405.5 2.1 fusion.239
  407.6 2.1 fusion.237
  411.0 2.1 constant_dynamic-update-slice_fusion.3
  415.4 2.1 fusion.238
  421.2 2.1 fusion.239
  423.4 2.1 fusion.237
  426.7 2.1 constant_dynamic-update-slice_fusion.3
  431.2 2.1 fusion.238
  437.0 2.1 fusion.239
  439.1 2.1 fusion.237
  442.5 2.1 constant_dynamic-update-slice_fusion.3
  447.0 2.1 fusion.238
  452.8 2.1 fusion.239
  454.9 2.1 fusion.237
  458.3 2.1 constant_dynamic-update-slice_fusion.3
  462.7 2.1 fusion.238
  468.5 2.1 fusion.239
  470.6 2.1 fusion.237
  474.0 2.1 constant_dynamic-update-slice_fusion.3
  476.1 7.3 multiply_reduce_fusion.1
  484.1 4.5 multiply_reduce_fusion
  488.6 6.6 fusion.137
  495.2 6.5 fusion.141
  501.7 2.9 collective-permute-start.4
  504.6 2.4 collective-permute-start.5
  507.1 5.6 fusion.140
  512.7 8.2 fusion.43
  523.1 4.6 collective-permute-start.7
  529.3 9.1 %stack.199 = f32[49,256]{1,0:T(8,128)} concatenate(f32[1,256]{1,0:T(1,128)} %bitcast.434, f32[1,256]{1,0:T(1,128)} %bitcast.433, f32[1,256]{1,0:T(1,128)} %bitcast.432, f32[1,256]{1,0:T(1,128)} %bitcast.428, f32[1,256]{1,0:T(1,128)} %bitcast.424, f32[1,256]{1,0:T(1,128)} %bitcast.423, f32[1,256]{1,0:T(1,128)} %bitcast.405, f32[1,256]{1,0:T(1,128)S(1)} %bitcast.387, ...), dimensions={0} | concatenate | bytes 100352 | tf_op jit(solution)/shard_map/stack | solution.py:67
  540.9 21.4 %convert_reduce_fusion = (f32[256]{0:T(256)}, bf16[32,64,256]{2,1,0:T(8,128)(2,1)S(1)}) fusion(f32[256]{0:T(256)} %bitcast.383, bf16[38,67,256]{2,1,0:T(8,128)(2,1)S(1)} %get-tuple-element.251, f32[256]{0:T(256)} %bitcast.385, f32[256]{0:T(256)S(1)} %bitcast.291, f32[256]{0:T(256)S(1)} %bitcast.293, bf16[32,64,256]{2,1,0:T(8,128)(2,1)S(1)} %get-tuple-element.239, ...), kind=kLoop, calls=%fused_computation.283 | loop fusion | flops 81788672 | bytes 46385152 | tf_op jit(solution)/shard_map/reduce_sum | solution.py:196
  564.8 79.6 %all-reduce.12.cloned.1.call-done = (f32[256]{0:T(256)}, f32[49,256]{1,0:T(8,128)}, f32[48,256]{1,0:T(8,128)}, f32[256]{0:T(256)}) async-done(((f32[256]{0:T(256)}, f32[49,256]{1,0:T(8,128)}, f32[48,256]{1,0:T(8,128)}, f32[256]{0:T(256)}), (f32[256]{0:T(256)}, f32[49,256]{1,0:T(8,128)}, f32[48,256]{1,0:T(8,128)}, f32[256]{0:T(256)})) %all-reduce.12.cloned.1.call-update) | async-done | bytes 101392 | tf_op jit(solution)/shard_map/psum | solution.py:200
  644.4 100.0 %all-reduce.14.cloned.1.call-done = (f32[256,1024]{1,0:T(8,128)}, f32[256,2048]{1,0:T(8,128)}) async-done(((f32[256,1024]{1,0:T(8,128)}, f32[256,2048]{1,0:T(8,128)}), (f32[256,1024]{1,0:T(8,128)}, f32[256,2048]{1,0:T(8,128)})) %all-reduce.14.cloned.1.call-update) | async-done | bytes 3145744 | tf_op jit(solution)/shard_map/psum | solution.py:200
  748.2 55.6 %all-reduce.16.cloned.1.call-done = (f32[256]{0:T(256)}, f32[49,256]{1,0:T(8,128)}, f32[48,256]{1,0:T(8,128)}, f32[256]{0:T(256)}) async-done(((f32[256]{0:T(256)}, f32[49,256]{1,0:T(8,128)}, f32[48,256]{1,0:T(8,128)}, f32[256]{0:T(256)}), (f32[256]{0:T(256)}, f32[49,256]{1,0:T(8,128)}, f32[48,256]{1,0:T(8,128)}, f32[256]{0:T(256)})) %all-reduce.16.cloned.1.call-update) | async-done | bytes 101392 | tf_op jit(solution)/shard_map/psum | solution.py:200
  803.7 70.3 %all-reduce.18.cloned.1.call-done = (f32[256,1024]{1,0:T(8,128)}, f32[256,2048]{1,0:T(8,128)}) async-done(((f32[256,1024]{1,0:T(8,128)}, f32[256,2048]{1,0:T(8,128)}), (f32[256,1024]{1,0:T(8,128)}, f32[256,2048]{1,0:T(8,128)})) %all-reduce.18.cloned.1.call-update) | async-done | bytes 3145744 | tf_op jit(solution)/shard_map/psum | solution.py:200
  874.0 2.5 copy.93
  (405 shorter events, 132.3 us)
Async XLA Ops:
  7.2 62.4 %copy-start = (bf16[256,2048]{1,0:T(8,128)(2,1)S(1)}, bf16[256,2048]{1,0:T(8,128)(2,1)}, u32[]{:S(2)}) copy-start(bf16[256,2048]{1,0:T(8,128)(2,1)} %param.17) | copy-start | bytes 3145732
  7.2 338.3 %all-reduce.10.cloned.1.call-start = ((), (), s32[]{:S(2)}) async-start(), calls=%async_computation | async-start | bytes 2097152 | tf_op jit(solution)/shard_map/psum | solution.py:157
  22.6 6.4 copy-start.33
  22.6 6.4 copy-start.121
  28.6 7.8 copy-start.30
  28.6 14.8 %copy-start.25 = (bf16[256,1024]{1,0:T(8,128)(2,1)S(1)}, bf16[256,1024]{1,0:T(8,128)(2,1)}, u32[]{:S(2)}) copy-start(bf16[256,1024]{1,0:T(8,128)(2,1)} %param.18) | copy-start | bytes 1572868
  29.0 14.4 %copy-start.13 = (bf16[2048,48]{0,1:T(8,128)(2,1)}, bf16[2048,48]{0,1:T(8,128)(2,1)S(1)}, u32[]{:S(2)}) copy-start(bf16[2048,48]{0,1:T(8,128)(2,1)S(1)} %reshape.155) | copy-start | bytes 589828
  29.5 19.1 %copy-start.5 = (bf16[2048,256]{1,0:T(8,128)(2,1)}, bf16[2048,256]{1,0:T(8,128)(2,1)S(1)}, u32[]{:S(2)}) copy-start(bf16[2048,256]{1,0:T(8,128)(2,1)S(1)} %fusion.44) | copy-start | bytes 3145732
  29.5 8.2 collective-permute-start.1
  32.8 5.2 collective-permute-start
  37.7 5.7 copy-start.15
  38.0 5.4 copy-start.18
  38.1 6.9 collective-permute-start.2
  41.3 5.6 collective-permute-start.3
  44.7 3.9 copy-start.37
  44.7 3.9 copy-start.39
  44.7 3.9 copy-start.41
  44.7 3.9 copy-start.43
  44.7 3.9 copy-start.45
  44.7 3.9 copy-start.47
  44.7 3.9 copy-start.49
  44.7 3.9 copy-start.51
  44.7 3.9 copy-start.53
  44.7 3.9 copy-start.55
  44.8 3.9 copy-start.57
  44.8 3.9 copy-start.59
  44.8 3.9 copy-start.61
  44.8 3.9 copy-start.63
  44.8 3.9 copy-start.65
  44.8 3.9 copy-start.67
  44.8 3.9 copy-start.69
  44.8 3.9 copy-start.71
  48.5 19.6 %copy-start.1 = (bf16[38,67,256]{2,1,0:T(8,128)(2,1)}, bf16[38,67,256]{2,1,0:T(8,128)(2,1)S(1)}, u32[]{:S(2)}) copy-start(bf16[38,67,256]{2,1,0:T(8,128)(2,1)S(1)} %get-tuple-element.255) | copy-start | bytes 3910660
  200.6 443.8 %all-reduce.12.cloned.1.call-start = ((), (), s32[]{:S(2)}) async-start(), calls=%async_computation.1 | async-start | bytes 217088 | tf_op jit(solution)/shard_map/psum | solution.py:200
  476.1 8.0 copy-start.109
  484.1 4.5 copy-start.4
  484.1 4.5 copy-start.7
  484.1 4.5 copy-start.27
  488.6 6.6 copy-start.2
  495.2 11.9 %copy-start.6 = (bf16[2048,256]{1,0:T(8,128)(2,1)S(1)}, bf16[2048,256]{1,0:T(8,128)(2,1)}, u32[]{:S(2)}) copy-start(bf16[2048,256]{1,0:T(8,128)(2,1)} %copy-done.5) | copy-start | bytes 3145732
  495.2 11.9 %copy-start.17 = (bf16[3,64,256]{2,1,0:T(8,128)(2,1)S(1)}, bf16[3,64,256]{2,1,0:T(8,128)(2,1)}, u32[]{:S(2)}) copy-start(bf16[3,64,256]{2,1,0:T(8,128)(2,1)} %copy-done.15) | copy-start | bytes 294916
  495.2 11.9 %copy-start.20 = (bf16[3,64,256]{2,1,0:T(8,128)(2,1)S(1)}, bf16[3,64,256]{2,1,0:T(8,128)(2,1)}, u32[]{:S(2)}) copy-start(bf16[3,64,256]{2,1,0:T(8,128)(2,1)} %copy-done.18) | copy-start | bytes 294916
  495.2 17.5 %copy-start.123 = (bf16[8,2048,128]{1,2,0:T(8,128)(2,1)S(1)}, bf16[8,2048,128]{1,2,0:T(8,128)(2,1)}, u32[]{:S(2)}) copy-start(bf16[8,2048,128]{1,2,0:T(8,128)(2,1)} %get-tuple-element.109) | copy-start | bytes 12582916
  501.7 19.3 %collective-permute-start.4 = (bf16[3,64,256]{2,1,0:T(8,128)(2,1)S(1)}, bf16[3,64,256]{2,1,0:T(8,128)(2,1)S(1)}, u32[]{:S(2)}, u32[]{:S(2)}) collective-permute-start(bf16[3,64,256]{2,1,0:T(8,128)(2,1)S(1)} %get-tuple-element.258), channel_id=1, source_target_pairs={{0,16},{16,32},{32,48},{48,64},{64,80},{80,96},{96,112},{1,17},{17... | collective-permute-start | bytes 294920 | tf_op jit(solution)/shard_map/ppermute | solution.py:20
  504.6 8.1 copy-start.9
  504.6 8.1 copy-start.122
  504.6 16.4 %collective-permute-start.5 = (bf16[3,64,256]{2,1,0:T(8,128)(2,1)S(1)}, bf16[3,64,256]{2,1,0:T(8,128)(2,1)S(1)}, u32[]{:S(2)}, u32[]{:S(2)}) collective-permute-start(bf16[3,64,256]{2,1,0:T(8,128)(2,1)S(1)} %get-tuple-element.259), channel_id=1, source_target_pairs={{16,0},{32,16},{48,32},{64,48},{80,64},{96,80},{112,96},{17,1},{33... | collective-permute-start | bytes 294920 | tf_op jit(solution)/shard_map/ppermute | solution.py:21
  521.0 8.3 copy-start.21
  521.0 8.3 copy-start.23
  521.7 17.1 %collective-permute-start.6 = (bf16[38,3,256]{2,1,0:T(4,128)(2,1)}, bf16[38,3,256]{2,1,0:T(4,128)(2,1)}, u32[]{:S(2)}, u32[]{:S(2)}) collective-permute-start(bf16[38,3,256]{2,1,0:T(4,128)(2,1)} %get-tuple-element.252), channel_id=1, source_target_pairs={{1,0},{2,1},{3,2},{4,3},{5,4},{6,5},{7,6},{8,7},{9,8},{10,9},{11,1... | collective-permute-start | bytes 175112 | tf_op jit(solution)/shard_map/ppermute | solution.py:21
  523.0 6.2 copy-start.110
  523.0 6.2 copy-start.111
  523.1 6.2 copy-start.112
  523.1 6.2 copy-start.113
  523.1 6.2 copy-start.114
  523.1 6.2 copy-start.115
  523.1 6.2 copy-start.116
  523.1 6.2 copy-start.117
  523.1 6.2 copy-start.118
  523.1 15.7 %collective-permute-start.7 = (bf16[38,3,256]{2,1,0:T(4,128)(2,1)}, bf16[38,3,256]{2,1,0:T(4,128)(2,1)}, u32[]{:S(2)}, u32[]{:S(2)}) collective-permute-start(bf16[38,3,256]{2,1,0:T(4,128)(2,1)} %get-tuple-element.253), channel_id=1, source_target_pairs={{0,1},{1,2},{2,3},{3,4},{4,5},{5,6},{6,7},{7,8},{8,9},{9,10},{10,1... | collective-permute-start | bytes 175112 | tf_op jit(solution)/shard_map/ppermute | solution.py:20
  540.9 21.4 %copy-start.14 = (bf16[2048,48]{0,1:T(8,128)(2,1)S(1)}, bf16[2048,48]{0,1:T(8,128)(2,1)}, u32[]{:S(2)}) copy-start(bf16[2048,48]{0,1:T(8,128)(2,1)} %copy-done.13) | copy-start | bytes 589828
  563.3 181.1 %all-reduce.14.cloned.1.call-start = ((), (), s32[]{:S(2)}) async-start(), calls=%async_computation.2 | async-start | bytes 6291456 | tf_op jit(solution)/shard_map/psum | solution.py:200
  564.7 239.0 %all-reduce.16.cloned.1.call-start = ((), (), s32[]{:S(2)}) async-start(), calls=%async_computation.3 | async-start | bytes 217088 | tf_op jit(solution)/shard_map/psum | solution.py:200
  644.4 229.6 %all-reduce.18.cloned.1.call-start = ((), (), s32[]{:S(2)}) async-start(), calls=%async_computation.4 | async-start | bytes 6291456 | tf_op jit(solution)/shard_map/psum | solution.py:200
  (73 other events, 187.8 us)
Sparse Core Ops, SparseCore 0:
  200.7 144.7 all-reduce.9
  563.4 80.8 all-reduce.11
  648.4 95.9 all-reduce.13
  746.8 56.8 all-reduce.15
  806.2 67.7 all-reduce.17
